TPU v7x, 32 devices: a whole 2x2x4 slice. The times are simulated.
32 devices in a mesh: row: 4 (over y, x), col: 8 (over z, core).
Axes of the slice: x: 2, y: 2, z: 4, core: 2. Of those that a mesh axis runs over, the one named last changes fastest.
Arguments:
- loads: float32 [4, 8, 1024, 8], P('row', 'col'), may hold values from -6 to 6
- schur: float32 [4, 8, 1024, 1024], P('row', 'col'), may hold values from -0.5 to 4.5, as said below
- factor: float32 [4, 8, 1024, 1024], P('row', 'col'), may hold values from -0.5 to 0.6, as said below
- coarse_inverse: float32 [1536, 1536], P(('row', 'col')), may hold values from -0.5 to 1.5, as said below
- elements: int32 [4, 8], P('row', 'col'), may hold values from 4096 to 16383
- west_map: int32 [4, 8, 256], P('row', 'col'), may hold values from 0 to 255, each once within a row
- south_map: int32 [4, 8, 256], P('row', 'col'), may hold values from 0 to 255, each once within a row
- prim_local: int32 [4, 8, 48], P('row', 'col'), may hold values from 0 to 1023
- prim_coarse: int32 [4, 8, 48], P('row', 'col'), may hold values from 0 to 1535
Outputs:
- solution: float32 [4, 8, 1024, 8], P('row', 'col')
- residual: float32 [4, 8, 1024, 8], P('row', 'col')
Inputs may be any that keep to these rules, and one draw needn't show every extreme that they name: `schur`: symmetric positive definite. `factor`: symmetric positive definite. `coarse_inverse`: symmetric positive definite. `west_map`: each subdomain's row is a permutation of 0 to 255. `south_map`: each subdomain's row is a permutation of 0 to 255. `prim_local`: values may repeat. `prim_coarse`: values may repeat, within a subdomain and between subdomains.
All inputs are finite; a program needn't handle non-finite values.
Results may differ from a plain program's by a relative error of at most 0.0001.
Values sent between devices are 32-bit elements; how exact they have to be, the bound alone decides.
A program may use at most 128 MiB of HBM per device.

v0:
```python
import jax
import jax.numpy as jnp
from jax import lax
from jax.sharding import PartitionSpec as P

ELEM_BASE = 4096


HIGHEST_PRECISION = lax.Precision.HIGHEST


def from_behind(x, axis, by):
    devices = lax.axis_size(axis)
    pairs = [(i, i + by) for i in range(devices) if 0 <= i + by < devices]
    return lax.ppermute(x, axis, pairs)


def product(matrix, vectors):
    return jnp.dot(matrix, vectors, precision=HIGHEST_PRECISION, preferred_element_type=jnp.float32)


def body(
    loads, schur, factor, coarse_inverse, elements, west_map, south_map, prim_local, prim_coarse
):
    schur_block = schur[0, 0]
    factor_block = factor[0, 0]
    local_loads = loads[0, 0]
    sweep_count = elements[0, 0] // ELEM_BASE
    west_order = west_map[0, 0]
    south_order = south_map[0, 0]
    primal_local = prim_local[0, 0]
    primal_coarse = prim_coarse[0, 0]
    unknowns = schur_block.shape[0]
    face_size = unknowns // 4
    column = lax.axis_index("col")
    grid_row = lax.axis_index("row")
    neighbour_flags = jnp.stack(
        [
            column > 0,
            column < lax.axis_size("col") - 1,
            grid_row > 0,
            grid_row < lax.axis_size("row") - 1,
        ]
    )
    weights = jnp.where(neighbour_flags[jnp.arange(unknowns) // face_size], 0.5, 1.0).astype(
        jnp.float32
    )[:, None]

    def assemble(values):
        west_face = values[:face_size]
        east_face = values[face_size : 2 * face_size]
        south_face = values[2 * face_size : 3 * face_size]
        north_face = values[3 * face_size :]
        from_west = from_behind(east_face, "col", 1)
        west_add = jnp.take(from_west, west_order, axis=0)
        west_back = jnp.zeros_like(west_face).at[west_order].set(west_face)
        from_east = from_behind(west_back, "col", -1)
        from_south = from_behind(north_face, "row", 1)
        south_add = jnp.take(from_south, south_order, axis=0)
        south_back = jnp.zeros_like(south_face).at[south_order].set(south_face)
        from_north = from_behind(south_back, "row", -1)
        return values + jnp.concatenate([west_add, from_east, south_add, from_north], axis=0)

    def weighted_sum(first, second):
        return jnp.sum(weights * first * second, axis=0)

    all_primal = lax.all_gather(primal_coarse, ("row", "col"), axis=0, tiled=True)
    right_side = assemble(local_loads)
    residual = right_side
    scaled = weights * residual
    local = product(factor_block, scaled)

    def sweep(turn, present):
        return present + product(factor_block, scaled - product(schur_block, present))

    local = lax.fori_loop(1, sweep_count, sweep, local)
    picked = jnp.take(scaled, primal_local, axis=0)
    columns = jnp.take(coarse_inverse, all_primal, axis=1)
    solved = product(columns, lax.all_gather(picked, ("row", "col"), axis=0, tiled=True))
    whole = lax.all_gather(solved, ("row", "col"), axis=0, tiled=True)
    precond = assemble(
        weights
        * (
            local
            + jnp.zeros_like(scaled).at[primal_local].add(jnp.take(whole, primal_coarse, axis=0))
        )
    )
    product_now = lax.psum(weighted_sum(residual, precond), ("row", "col"))
    image = assemble(product(schur_block, precond))
    alpha = product_now / lax.psum(weighted_sum(precond, image), ("row", "col"))
    solution = alpha * precond
    residual = residual - alpha * image
    return (solution[None, None], residual[None, None])


def solution(mesh):
    placed = (
        P("row", "col", None, None),
        P("row", "col", None, None),
        P("row", "col", None, None),
        P(("row", "col"), None),
        P("row", "col"),
        P("row", "col", None),
        P("row", "col", None),
        P("row", "col", None),
        P("row", "col", None),
    )
    return jax.shard_map(
        body,
        mesh=mesh,
        in_specs=placed,
        out_specs=(P("row", "col", None, None), P("row", "col", None, None)),
        check_vma=False,
    )
```

profile of v0, /device:TPU:0, one launch (start us, length us, event | category | flops | bytes accessed | tf_op | source)
XLA Modules:
  0.0 256.3 jit_solution(8718719181798448319)
XLA Ops:
  3.5 1.3 collective-permute-start.1
  6.8 1.3 collective-permute-start.3
  8.3 5.5 %collective-permute-start.2 = (f32[256,8]{1,0:T(8,128)S(1)}, f32[256,8]{1,0:T(8,128)S(1)}, u32[]{:S(2)}, u32[]{:S(2)}) collective-permute-start(f32[256,8]{1,0:T(8,128)S(1)} %bitcast.105), channel_id=1, source_target_pairs={{0,8},{8,16},{16,24},{1,9},{9,17},{17,25},{2,10},{10,18},{18,26},{... | collective-permute-start | bytes 24584 | tf_op jit(solution)/shard_map/ppermute | solution.py:15
  13.9 2.8 %collective-permute-start = (f32[256,8]{1,0:T(8,128)S(1)}, f32[256,8]{1,0:T(8,128)S(1)}, u32[]{:S(2)}, u32[]{:S(2)}) collective-permute-start(f32[256,8]{1,0:T(8,128)S(1)} %bitcast.104), channel_id=1, source_target_pairs={{0,1},{1,2},{2,3},{3,4},{4,5},{5,6},{6,7},{8,9},{9,10},{10,11},{11... | collective-permute-start | bytes 24584 | tf_op jit(solution)/shard_map/ppermute | solution.py:15
  22.8 41.8 %all-reduce = s32[1536]{0:T(1024)S(1)} all-reduce(s32[1536]{0:T(1024)S(1)} %bitcast_dynamic-update-slice_fusion), channel_id=2, replica_groups=mesh['row'=4,'col'=8] {'row','col'}, use_global_device_ids=true, to_apply=%add | all-reduce | flops 1536 | bytes 12288 | tf_op jit(solution)/shard_map/all_gather | solution.py:67
  65.4 1.2 copy.96
  66.6 2.6 %gather_fusion = f32[1536,48]{1,0:T(8,128)S(1)} fusion(f32[48,1536]{0,1:T(8,128)S(1)} %copy.96, s32[2048]{0:T(1024)S(1)} %pad_clamp_fusion), kind=kCustom, calls=%fused_computation.6 | custom fusion | bytes 595968 | tf_op jit(solution)/shard_map/jit(_take)/gather | solution.py:78
  71.1 5.7 %convolution_bitcast_fusion.2 = f32[1024,8]{0,1:T(8,128)S(1)} fusion(f32[1,1,1024,8]{2,3,1,0:T(8,128)S(1)} %copy-done.1, f32[1,1,256,8]{2,3,1,0:T(8,128)S(1)} %bitcast.107, f32[1,1,256,8]{2,3,1,0:T(8,128)S(1)} %bitcast.102, f32[1,1,256,8]{2,3,1,0:T(8,128)S(1)} %bitcast.106, f32[1,1,256,8]{2,3,1,0:T(8,128)S(1)} %bitcast.103, f32[1024]{0:T(1024)S(1)} %bitcast.98, ...), kind=kOutput, calls=%fused_computation.20 | convolution fusion | flops 100704256 | bytes 4296704 | tf_op jit(solution)/shard_map/dot_general | solution.py:19
  76.8 9.6 %while.10 = (s32[]{:T(128)}, f32[1024,8]{0,1:T(8,128)S(1)}, s32[]{:T(128)}, f32[1024,1024]{1,0:T(8,128)}, f32[1024,8]{0,1:T(8,128)S(1)}, /*index=5*/f32[1024,1024]{1,0:T(8,128)}, s32[]{:T(128)}) while((s32[]{:T(128)}, f32[1024,8]{0,1:T(8,128)S(1)}, s32[]{:T(128)}, f32[1024,1024]{1,0:T(8,128)}, f32[1024,8]{0,1:T(8,128)S(1)}, ...), condition=%wide.region_3.5_spmd, body=%wide.region_2.4_spmd.sunk | while | flops 201342976 | bytes 25362536 | solution.py:76
  76.9 5.9 %convolution_subtract_fusion.2 = f32[1024,8]{0,1:T(8,128)S(1)} fusion(f32[1024,8]{0,1:T(8,128)S(1)} %get-tuple-element.125, f32[1024,1024]{1,0:T(8,128)} %get-tuple-element.124, f32[1024,8]{0,1:T(8,128)S(1)} %get-tuple-element.115), kind=kOutput, calls=%fused_computation.18.clone.1 | convolution fusion | flops 100671488 | bytes 4292608 | tf_op jit(solution)/shard_map/while/body/dot_general | solution.py:19
  82.8 3.6 %fusion.55 = f32[1024,8]{0,1:T(8,128)S(1)} fusion(f32[1024,8]{0,1:T(8,128)S(1)} %get-tuple-element.115, f32[1024,8]{0,1:T(8,128)S(1)} %convolution_subtract_fusion.2, f32[1024,1024]{1,0:T(8,128)S(1)} %copy-done), kind=kOutput, calls=%fused_computation.17.clone.1 | convolution fusion | flops 100671488 | bytes 4292608 | tf_op jit(solution)/shard_map/while/body/dot_general | solution.py:19
  87.3 46.5 %all-gather.1 = f32[32,48,8]{1,2,0:T(8,128)S(1)} all-gather(f32[1,48,8]{1,2,0:T(8,128)S(1)} %copy.98), channel_id=1, replica_groups=mesh['row'=4,'col'=8] {'row','col'}, dimensions={0}, use_global_device_ids=true | all-gather | bytes 50688 | tf_op jit(solution)/shard_map/all_gather | solution.py:79
  134.6 37.2 %all-gather.2 = f32[32,48,8]{1,2,0:T(8,128)S(1)} all-gather(f32[1,48,8]{1,2,0:T(8,128)S(1)} %convolution_bitcast_fusion.3), channel_id=1, replica_groups=mesh['row'=4,'col'=8] {'row','col'}, dimensions={0}, use_global_device_ids=true | all-gather | bytes 50688 | tf_op jit(solution)/shard_map/all_gather | solution.py:80
  173.4 1.3 collective-permute-start.6
  174.7 2.2 collective-permute-start.4
  178.4 1.3 collective-permute-start.7
  181.0 1.5 collective-permute-start.5
  184.5 4.5 %collective-permute-done.7 = f32[256,8]{0,1:T(8,128)S(1)} collective-permute-done((f32[256,8]{0,1:T(8,128)S(1)}, f32[256,8]{0,1:T(8,128)S(1)}, u32[]{:S(2)}, u32[]{:S(2)}) %collective-permute-start.7) | collective-permute-done | bytes 8224 | tf_op jit(solution)/shard_map/ppermute | solution.py:15
  189.0 5.6 %convolution_bitcast_fusion.1 = f32[1024,8]{0,1:T(8,128)S(1)} fusion(f32[1024,8]{0,1:T(8,128)S(1)} %maximum_add_fusion.2, f32[1,1,1024,1024]{3,2,1,0:T(8,128)} %bitcast.95), kind=kOutput, calls=%fused_computation.19 | convolution fusion | flops 100663296 | bytes 4259840 | tf_op jit(solution)/shard_map/dot_general | solution.py:19
  194.6 5.9 %collective-permute-start.10 = (f32[256,8]{0,1:T(8,128)S(1)}, f32[256,8]{0,1:T(8,128)S(1)}, u32[]{:S(2)}, u32[]{:S(2)}) collective-permute-start(f32[256,8]{0,1:T(8,128)S(1)} %get-tuple-element.55), channel_id=1, source_target_pairs={{0,8},{8,16},{16,24},{1,9},{9,17},{17,25},{2,10},{10,18},{18,26},{... | collective-permute-start | bytes 24584 | tf_op jit(solution)/shard_map/ppermute | solution.py:15
  200.6 4.0 %collective-permute-start.8 = (f32[256,8]{0,1:T(8,128)S(1)}, f32[256,8]{0,1:T(8,128)S(1)}, u32[]{:S(2)}, u32[]{:S(2)}) collective-permute-start(f32[256,8]{0,1:T(8,128)S(1)} %get-tuple-element.53), channel_id=1, source_target_pairs={{0,1},{1,2},{2,3},{3,4},{4,5},{5,6},{6,7},{8,9},{9,10},{10,11},{11... | collective-permute-start | bytes 24584 | tf_op jit(solution)/shard_map/ppermute | solution.py:15
  206.0 1.3 collective-permute-start.11
  208.7 1.3 collective-permute-start.9
  212.5 43.1 %all-reduce.1 = (f32[8]{0:T(128)S(1)}, f32[8]{0:T(128)S(1)}) all-reduce(f32[8]{0:T(128)S(1)} %get-tuple-element.38, f32[8]{0:T(128)S(1)} %get-tuple-element.37), channel_id=1, replica_groups=mesh['row'=4,'col'=8] {'row','col'}, use_global_device_ids=true, to_apply=%region_8.10 | all-reduce | flops 16 | bytes 128 | tf_op jit(solution)/shard_map/psum | solution.py:88
  (96 shorter events, 27.0 us)
Async XLA Ops:
  0.6 70.3 %copy-start.1 = (f32[1,1,1024,8]{2,3,1,0:T(8,128)S(1)}, f32[1,1,1024,8]{2,3,1,0:T(8,128)}, u32[]{:S(2)}) copy-start(f32[1,1,1024,8]{2,3,1,0:T(8,128)} %param.13) | copy-start | bytes 98308
  3.5 67.4 %collective-permute-start.1 = (f32[256,8]{0,1:T(8,128)S(1)}, f32[256,8]{0,1:T(8,128)S(1)}, u32[]{:S(2)}, u32[]{:S(2)}) collective-permute-start(f32[256,8]{0,1:T(8,128)S(1)} %copy.91), channel_id=1, source_target_pairs={{1,0},{2,1},{3,2},{4,3},{5,4},{6,5},{7,6},{9,8},{10,9},{11,10},{12... | collective-permute-start | bytes 24584 | tf_op jit(solution)/shard_map/ppermute | solution.py:15
  6.8 64.0 %collective-permute-start.3 = (f32[256,8]{0,1:T(8,128)S(1)}, f32[256,8]{0,1:T(8,128)S(1)}, u32[]{:S(2)}, u32[]{:S(2)}) collective-permute-start(f32[256,8]{0,1:T(8,128)S(1)} %copy.95), channel_id=1, source_target_pairs={{8,0},{16,8},{24,16},{9,1},{17,9},{25,17},{10,2},{18,10},{26,18},{... | collective-permute-start | bytes 24584 | tf_op jit(solution)/shard_map/ppermute | solution.py:15
  8.3 61.0 %collective-permute-start.2 = (f32[256,8]{1,0:T(8,128)S(1)}, f32[256,8]{1,0:T(8,128)S(1)}, u32[]{:S(2)}, u32[]{:S(2)}) collective-permute-start(f32[256,8]{1,0:T(8,128)S(1)} %bitcast.105), channel_id=1, source_target_pairs={{0,8},{8,16},{16,24},{1,9},{9,17},{17,25},{2,10},{10,18},{18,26},{... | collective-permute-start | bytes 24584 | tf_op jit(solution)/shard_map/ppermute | solution.py:15
  13.9 56.1 %collective-permute-start = (f32[256,8]{1,0:T(8,128)S(1)}, f32[256,8]{1,0:T(8,128)S(1)}, u32[]{:S(2)}, u32[]{:S(2)}) collective-permute-start(f32[256,8]{1,0:T(8,128)S(1)} %bitcast.104), channel_id=1, source_target_pairs={{0,1},{1,2},{2,3},{3,4},{4,5},{5,6},{6,7},{8,9},{9,10},{10,11},{11... | collective-permute-start | bytes 24584 | tf_op jit(solution)/shard_map/ppermute | solution.py:15
  76.9 5.9 %copy-start = (f32[1024,1024]{1,0:T(8,128)S(1)}, f32[1024,1024]{1,0:T(8,128)}, u32[]{:S(2)}) copy-start(f32[1024,1024]{1,0:T(8,128)} %get-tuple-element.126) | copy-start | bytes 12582916 | tf_op jit(solution)/shard_map/while
  173.4 9.1 %collective-permute-start.6 = (f32[256,8]{0,1:T(8,128)S(1)}, f32[256,8]{0,1:T(8,128)S(1)}, u32[]{:S(2)}, u32[]{:S(2)}) collective-permute-start(f32[256,8]{0,1:T(8,128)S(1)} %get-tuple-element.59), channel_id=1, source_target_pairs={{0,8},{8,16},{16,24},{1,9},{9,17},{17,25},{2,10},{10,18},{18,26},{... | collective-permute-start | bytes 24584 | tf_op jit(solution)/shard_map/ppermute | solution.py:15
  174.7 8.8 %collective-permute-start.4 = (f32[256,8]{0,1:T(8,128)S(1)}, f32[256,8]{0,1:T(8,128)S(1)}, u32[]{:S(2)}, u32[]{:S(2)}) collective-permute-start(f32[256,8]{0,1:T(8,128)S(1)} %get-tuple-element.57), channel_id=1, source_target_pairs={{0,1},{1,2},{2,3},{3,4},{4,5},{5,6},{6,7},{8,9},{9,10},{10,11},{11... | collective-permute-start | bytes 24584 | tf_op jit(solution)/shard_map/ppermute | solution.py:15
  178.4 10.6 %collective-permute-start.7 = (f32[256,8]{0,1:T(8,128)S(1)}, f32[256,8]{0,1:T(8,128)S(1)}, u32[]{:S(2)}, u32[]{:S(2)}) collective-permute-start(f32[256,8]{0,1:T(8,128)S(1)} %copy.111), channel_id=1, source_target_pairs={{8,0},{16,8},{24,16},{9,1},{17,9},{25,17},{10,2},{18,10},{26,18},{... | collective-permute-start | bytes 24584 | tf_op jit(solution)/shard_map/ppermute | solution.py:15
  181.0 7.9 %collective-permute-start.5 = (f32[256,8]{0,1:T(8,128)S(1)}, f32[256,8]{0,1:T(8,128)S(1)}, u32[]{:S(2)}, u32[]{:S(2)}) collective-permute-start(f32[256,8]{0,1:T(8,128)S(1)} %copy.107), channel_id=1, source_target_pairs={{1,0},{2,1},{3,2},{4,3},{5,4},{6,5},{7,6},{9,8},{10,9},{11,10},{12... | collective-permute-start | bytes 24584 | tf_op jit(solution)/shard_map/ppermute | solution.py:15
  194.6 15.4 %collective-permute-start.10 = (f32[256,8]{0,1:T(8,128)S(1)}, f32[256,8]{0,1:T(8,128)S(1)}, u32[]{:S(2)}, u32[]{:S(2)}) collective-permute-start(f32[256,8]{0,1:T(8,128)S(1)} %get-tuple-element.55), channel_id=1, source_target_pairs={{0,8},{8,16},{16,24},{1,9},{9,17},{17,25},{2,10},{10,18},{18,26},{... | collective-permute-start | bytes 24584 | tf_op jit(solution)/shard_map/ppermute | solution.py:15
  200.6 10.4 %collective-permute-start.8 = (f32[256,8]{0,1:T(8,128)S(1)}, f32[256,8]{0,1:T(8,128)S(1)}, u32[]{:S(2)}, u32[]{:S(2)}) collective-permute-start(f32[256,8]{0,1:T(8,128)S(1)} %get-tuple-element.53), channel_id=1, source_target_pairs={{0,1},{1,2},{2,3},{3,4},{4,5},{5,6},{6,7},{8,9},{9,10},{10,11},{11... | collective-permute-start | bytes 24584 | tf_op jit(solution)/shard_map/ppermute | solution.py:15
  206.0 6.2 %collective-permute-start.11 = (f32[256,8]{0,1:T(8,128)S(1)}, f32[256,8]{0,1:T(8,128)S(1)}, u32[]{:S(2)}, u32[]{:S(2)}) collective-permute-start(f32[256,8]{0,1:T(8,128)S(1)} %copy.119), channel_id=1, source_target_pairs={{8,0},{16,8},{24,16},{9,1},{17,9},{25,17},{10,2},{18,10},{26,18},{... | collective-permute-start | bytes 24584 | tf_op jit(solution)/shard_map/ppermute | solution.py:15
  208.7 3.7 %collective-permute-start.9 = (f32[256,8]{0,1:T(8,128)S(1)}, f32[256,8]{0,1:T(8,128)S(1)}, u32[]{:S(2)}, u32[]{:S(2)}) collective-permute-start(f32[256,8]{0,1:T(8,128)S(1)} %copy.115), channel_id=1, source_target_pairs={{1,0},{2,1},{3,2},{4,3},{5,4},{6,5},{7,6},{9,8},{10,9},{11,10},{12... | collective-permute-start | bytes 24584 | tf_op jit(solution)/shard_map/ppermute | solution.py:15
where the time goes:
time: 256 us
  blocking collectives  169 us (66%)
  starting transfers between devices  29.8 us (12%)
  matrix products  21.4 us (8%)
  local copies, waits for them, and re-layouts  20.7 us (8%)
  other arithmetic  8.95 us (3%)
  waiting for transfers between devices  5 us (2%)
    all_gather x1, blocking collectives, body(): lax.all_gather(picked, ('row', 'col'), axis=0, tiled=True)  46.5 us
    psum x1, blocking collectives, body(): product_now = lax.psum(weighted_sum(residual, precond), ('row', 'col'))  43.1 us
    all_gather x1, blocking collectives, body(): lax.all_gather(primal_coarse, ('row', 'col'), axis=0, tiled=True)  41.8 us
    all_gather x1, blocking collectives, body(): whole = lax.all_gather(solved, ('row', 'col'), axis=0, tiled=True)  37.2 us
    ppermute x12, starting transfers between devices, from_behind(): return lax.ppermute(x, axis, pairs)  29.8 us
    dot_general x5, matrix products, product(): jnp.dot(matrix, vectors, precision=HIGHEST_PRECISION, preferred_element_t...  21.4 us
  transfers between devices with their start and end apart: 12, of which 3 were waited for; matrix products, arithmetic and copies ran while one was open for 9% of the time, Pallas kernels for 0%

commit v1 on v0

v1 whole, which is shorter than its diff:
```python
import functools

import jax
import jax.numpy as jnp
from jax import lax
from jax.experimental import pallas as pl
from jax.experimental.pallas import tpu as pltpu
from jax.sharding import PartitionSpec as P

ELEM_BASE = 4096
MOST_SWEEPS = 3
MESH = pl.DeviceIdType.MESH
F32, BF16 = jnp.float32, jnp.bfloat16
NT = (((1,), (1,)), ((), ()))
IDX, RHS, SOL, SUM = range(4)


def split(values):
    high = values.astype(BF16).astype(F32)
    return jnp.concatenate([high, values - high], axis=0).astype(BF16)


def join(stacked):
    rows = stacked.shape[0] // 2
    return stacked[:rows] + stacked[rows:]


def dot(a, b):
    return jnp.dot(a, b, preferred_element_type=F32)


def dot_nt(a, b):
    return lax.dot_general(a, b, NT, preferred_element_type=F32)


def kernel(
    n_row, n_col, loads, schur_hbm, factor_hbm, coarse_hbm, elements, west_map, south_map,
    prim_local, prim_coarse, solution, residual,
    schur_in, factor_in, coarse_in, schur_hi, schur_lo, factor_hi, factor_lo,
    coarse_split, cols_hi, cols_lo, west_hot, south_hot, local_hot, coarse_hot,
    place, idx_row, idx_col, val_row, val_col, sum_row, sum_col,
    face_out, face_in, kept,
    copy_sem, face_send, face_recv, row_send, row_recv, col_send, col_recv,
):
    a, c = lax.axis_index("row"), lax.axis_index("col")
    unknowns = loads.shape[1]
    face = unknowns // 4
    wide = local_hot.shape[1]
    coarse_rows, coarse_all = coarse_in.shape
    nprim = prim_local.shape[1]

    copies = [
        pltpu.make_async_copy(src, dst, copy_sem.at[i])
        for i, (src, dst) in enumerate(
            [(factor_hbm, factor_in), (coarse_hbm, coarse_in), (schur_hbm, schur_in)]
        )
    ]
    barrier = pltpu.get_barrier_semaphore()
    for d in range(1, n_row):
        pl.semaphore_signal(barrier, inc=1, device_id=(lax.rem(a + d, n_row), c), device_id_type=MESH)
    for d in range(1, n_col):
        pl.semaphore_signal(barrier, inc=1, device_id=(a, lax.rem(c + d, n_col)), device_id_type=MESH)
    for copy in copies:
        copy.start()

    def hot(order_ref):
        return (
            lax.broadcasted_iota(jnp.int32, (face, face), 0) == order_ref[...]
        ).astype(F32).astype(BF16)

    west_hot[...] = hot(west_map)
    south_hot[...] = hot(south_map)

    def placed(source):
        place[...] = jnp.full(place.shape, -1, jnp.int32)
        place[:1, :nprim] = source[...]
        base = place[...]
        out = base
        for i in range(1, n_row):
            out = jnp.where(a == i, pltpu.roll(base, nprim * i, 1), out)
        return out[:1]

    own_coarse = placed(prim_coarse)
    own_local = placed(prim_local)
    idx_row[a] = own_coarse

    lane = lax.broadcasted_iota(jnp.int32, (1, unknowns), 1)
    flags = [c > 0, c < n_col - 1, a > 0, a < n_row - 1]
    halves = [jnp.where(flag, 0.5, 1.0).astype(F32) for flag in flags]
    weights = jnp.where(
        lane < face,
        halves[0],
        jnp.where(lane < 2 * face, halves[1], jnp.where(lane < 3 * face, halves[2], halves[3])),
    )
    targets = [(a, c + 1), (a, c - 1), (a + 1, c), (a - 1, c)]
    can_send = [flags[1], flags[0], flags[3], flags[2]]

    def face_copy(turn, slot):
        return pltpu.make_async_remote_copy(
            src_ref=face_out.at[turn, slot],
            dst_ref=face_in.at[turn, slot],
            send_sem=face_send.at[turn, slot],
            recv_sem=face_recv.at[turn, slot],
            device_id=targets[slot],
            device_id_type=MESH,
        )

    def face_fill(turn, values):
        face_out[turn, 0] = values[:, face : 2 * face]
        face_out[turn, 2] = values[:, 3 * face :]
        face_out[turn, 1] = join(dot_nt(split(values[:, :face]), west_hot[...]))
        face_out[turn, 3] = join(dot_nt(split(values[:, 2 * face : 3 * face]), south_hot[...]))

    def face_start(turn):
        for slot in range(4):
            @pl.when(can_send[slot])
            def _():
                face_copy(turn, slot).start()

    def face_finish(turn, values):
        for slot in range(4):
            @pl.when(flags[slot])
            def _():
                face_copy(turn, slot).wait_recv()

            @pl.when(jnp.logical_not(flags[slot]))
            def _():
                face_in[turn, slot] = jnp.zeros(face_in.shape[2:], F32)
        adds = [
            join(dot(split(face_in[turn, 0]), west_hot[...])),
            face_in[turn, 1],
            join(dot(split(face_in[turn, 2]), south_hot[...])),
            face_in[turn, 3],
        ]
        return values + jnp.concatenate(adds, axis=1)

    def spread(buffer, kind, along_row):
        n = n_row if along_row else n_col
        me = a if along_row else c
        sends, recvs = (row_send, row_recv) if along_row else (col_send, col_recv)
        out = []
        for d in range(1, n):
            peer = lax.rem(me + d, n)
            out.append(
                pltpu.make_async_remote_copy(
                    src_ref=buffer.at[me],
                    dst_ref=buffer.at[me],
                    send_sem=sends.at[kind, d],
                    recv_sem=recvs.at[kind, d],
                    device_id=(peer, c) if along_row else (a, peer),
                    device_id_type=MESH,
                )
            )
        return out

    started = []

    def start(group):
        for copy in group:
            copy.start()
        started.extend(group)
        return group

    def arrive(group):
        for copy in group:
            copy.wait_recv()

    def total(buffer, n):
        out = buffer[0]
        for i in range(1, n):
            out = out + buffer[i]
        return out

    first = loads[...]
    face_fill(0, first)
    pl.semaphore_wait(barrier, n_row + n_col - 2)
    face_start(0)
    idx_rows = start(spread(idx_row, IDX, True))

    rows_iota = lax.broadcasted_iota(jnp.int32, (unknowns, wide), 0)
    local_hot[...] = (rows_iota == own_local).astype(F32).astype(BF16)

    def split_matrix(source, high, low):
        step = 128

        def one(i, carry):
            at = pl.ds(pl.multiple_of(i * step, step), step)
            values = source[at, :]
            top = values.astype(BF16)
            high[at, :] = top
            low[at, :] = (values - top.astype(F32)).astype(BF16)
            return carry

        lax.fori_loop(0, source.shape[0] // step, one, 0)

    copies[0].wait()
    split_matrix(factor_in, factor_hi, factor_lo)

    arrive(idx_rows)
    merged = idx_row[0]
    for i in range(1, n_row):
        merged = jnp.maximum(merged, idx_row[i])
    idx_col[c] = merged
    idx_cols = start(spread(idx_col, IDX, False))

    right_side = face_finish(0, first)
    scaled = weights * right_side
    val_row[0, a] = join(dot(split(scaled), local_hot[...]))
    group = start(spread(val_row.at[0], RHS, True))

    def apply(high, low, vectors):
        both = split(vectors)
        return join(dot(both, high[...]) + dot(both, low[...]))

    local = apply(factor_hi, factor_lo, scaled)

    arrive(group)
    val_col[0, c] = total(val_row.at[0], n_row)
    group = start(spread(val_col.at[0], RHS, False))

    copies[1].wait()
    coarse_split[...] = split(coarse_in[...])
    arrive(idx_cols)
    chunk = 512 if coarse_all % 512 == 0 else 128

    def one_column(s, carry):
        wanted = idx_col[s]

        def one_chunk(k, acc):
            start_at = pl.multiple_of(k * chunk, chunk)
            here = lax.broadcasted_iota(jnp.int32, (chunk, wide), 0) + start_at
            picks = (here == wanted).astype(F32).astype(BF16)
            return acc + dot(coarse_split[:, pl.ds(start_at, chunk)], picks)

        acc = lax.fori_loop(
            0, coarse_all // chunk, one_chunk, jnp.zeros((2 * coarse_rows, wide), F32)
        )
        values = join(acc)
        top = values.astype(BF16)
        cols_hi[s] = top
        cols_lo[s] = (values - top.astype(F32)).astype(BF16)
        return carry

    lax.fori_loop(0, n_col, one_column, 0)

    arrive(group)
    solved = jnp.zeros((16, coarse_rows), F32)
    for s in range(n_col):
        terms = split(val_col[0, s])
        solved = solved + dot_nt(terms, cols_hi[s]) + dot_nt(terms, cols_lo[s])
    kept[...] = jnp.zeros(kept.shape, F32)
    kept[:, :coarse_rows] = join(solved)
    base = kept[...]
    moved = base
    for i in range(1, n_row):
        moved = jnp.where(a == i, pltpu.roll(base, coarse_rows * i, 1), moved)
    val_row[1, a] = moved
    group = start(spread(val_row.at[1], SOL, True))

    copies[2].wait()
    split_matrix(schur_in, schur_hi, schur_lo)

    def one_pick(s, carry):
        at = lax.broadcasted_iota(jnp.int32, (wide, wide), 0)
        block = jnp.zeros((wide, wide), jnp.int32)
        for i in range(1, n_row):
            block = block + (at >= coarse_rows * i).astype(jnp.int32)
        number = (block * n_col + s) * coarse_rows + at - block * coarse_rows
        number = jnp.where(at < n_row * coarse_rows, number, -2)
        coarse_hot[pl.ds(pl.multiple_of(s * wide, wide), wide), :] = (
            (number == own_coarse).astype(F32).astype(BF16)
        )
        return carry

    lax.fori_loop(0, n_col, one_pick, 0)

    arrive(group)
    val_col[1, c] = total(val_row.at[1], n_row)
    group = start(spread(val_col.at[1], SOL, False))

    for turn in range(2, MOST_SWEEPS + 1):
        inner = scaled - apply(schur_hi, schur_lo, local)
        later = local + apply(factor_hi, factor_lo, inner)
        more = jnp.broadcast_to(elements[...], local.shape) >= turn * ELEM_BASE
        local = jnp.where(more, later, local)

    arrive(group)
    read = jnp.zeros((16, wide), F32)
    for s in range(n_col):
        read = read + dot(split(val_col[1, s]), coarse_hot[s * wide : (s + 1) * wide, :])
    correction = join(dot_nt(split(join(read)), local_hot[...]))
    halved = weights * (local + correction)
    face_fill(1, halved)
    face_start(1)

    def lane_sum(values):
        return jnp.sum(values, axis=1, keepdims=True)

    rz = lane_sum(right_side * halved)
    precond = face_finish(1, halved)
    image = apply(schur_hi, schur_lo, precond)
    face_fill(2, image)
    face_start(2)
    pq = lane_sum(precond * image)
    sum_lane = lax.broadcasted_iota(jnp.int32, sum_row.shape[1:], 1)
    sum_row[a] = jnp.where(sum_lane == 0, rz, pq)
    group = start(spread(sum_row, SUM, True))
    arrive(group)
    sum_col[c] = total(sum_row, n_row)
    group = start(spread(sum_col, SUM, False))
    image = face_finish(2, image)
    arrive(group)
    sums = total(sum_col, n_col)
    alpha = sums[:, :1] / sums[:, 1:2]
    solution[...] = alpha * precond
    residual[...] = right_side - alpha * image

    for copy in started:
        copy.wait_send()
    for turn in range(3):
        for slot in range(4):
            @pl.when(can_send[slot])
            def _():
                face_copy(turn, slot).wait_send()


def up(n, to):
    return -(-n // to) * to


def body(
    n_row, n_col, loads, schur, factor, coarse_inverse, elements, west_map, south_map,
    prim_local, prim_coarse,
):
    vectors = loads[0, 0].T
    rhs, unknowns = vectors.shape
    face = unknowns // 4
    coarse_rows, coarse_all = coarse_inverse.shape
    nprim = prim_local.shape[2]
    wide = up(n_row * max(nprim, coarse_rows), 128)
    vmem = pl.BlockSpec(memory_space=pltpu.VMEM)
    hbm = pl.BlockSpec(memory_space=pl.ANY)
    dma = pltpu.SemaphoreType.DMA
    out = jax.ShapeDtypeStruct(vectors.shape, F32)
    solution, residual = pl.pallas_call(
        functools.partial(kernel, n_row, n_col),
        out_shape=(out, out),
        in_specs=[vmem, hbm, hbm, hbm, vmem, vmem, vmem, vmem, vmem],
        out_specs=(vmem, vmem),
        scratch_shapes=[
            pltpu.VMEM((unknowns, unknowns), F32),
            pltpu.VMEM((unknowns, unknowns), F32),
            pltpu.VMEM((coarse_rows, coarse_all), F32),
            pltpu.VMEM((unknowns, unknowns), BF16),
            pltpu.VMEM((unknowns, unknowns), BF16),
            pltpu.VMEM((unknowns, unknowns), BF16),
            pltpu.VMEM((unknowns, unknowns), BF16),
            pltpu.VMEM((2 * coarse_rows, coarse_all), BF16),
            pltpu.VMEM((n_col, coarse_rows, wide), BF16),
            pltpu.VMEM((n_col, coarse_rows, wide), BF16),
            pltpu.VMEM((face, face), BF16),
            pltpu.VMEM((face, face), BF16),
            pltpu.VMEM((unknowns, wide), BF16),
            pltpu.VMEM((n_col * wide, wide), BF16),
            pltpu.VMEM((8, wide), jnp.int32),
            pltpu.VMEM((n_row, 1, wide), jnp.int32),
            pltpu.VMEM((n_col, 1, wide), jnp.int32),
            pltpu.VMEM((2, n_row, rhs, wide), F32),
            pltpu.VMEM((2, n_col, rhs, wide), F32),
            pltpu.VMEM((n_row, rhs, 128), F32),
            pltpu.VMEM((n_col, rhs, 128), F32),
            pltpu.VMEM((3, 4, rhs, face), F32),
            pltpu.VMEM((3, 4, rhs, face), F32),
            pltpu.VMEM((rhs, wide), F32),
            dma((3,)),
            dma((3, 4)),
            dma((3, 4)),
            dma((4, n_row)),
            dma((4, n_row)),
            dma((4, n_col)),
            dma((4, n_col)),
        ],
        compiler_params=pltpu.CompilerParams(collective_id=0, has_side_effects=True),
    )(
        vectors, schur[0, 0], factor[0, 0], coarse_inverse, elements,
        west_map[0], south_map[0], prim_local[0], prim_coarse[0],
    )
    return solution.T[None, None], residual.T[None, None]


def solution(mesh):
    placed = (
        P("row", "col", None, None),
        P("row", "col", None, None),
        P("row", "col", None, None),
        P(("row", "col"), None),
        P("row", "col"),
        P("row", "col", None),
        P("row", "col", None),
        P("row", "col", None),
        P("row", "col", None),
    )
    return jax.shard_map(
        functools.partial(body, mesh.shape["row"], mesh.shape["col"]),
        mesh=mesh,
        in_specs=placed,
        out_specs=(P("row", "col", None, None), P("row", "col", None, None)),
        check_vma=False,
    )
```

time: 256 us -> 42.7 us (0.17)
  blocking collectives: 169 us -> 0 us
  Pallas kernels: 0 us -> 38.3 us
  starting transfers between devices: 29.8 us -> 0 us
  matrix products: 21.4 us -> 0 us
  local copies, waits for them, and re-layouts: 20.7 us -> 2.75 us
  other arithmetic: 8.95 us -> 0 us
  waiting for transfers between devices: 5 us -> 0 us
    all_gather x3 -> x0, blocking collectives: 126 us -> none  [the longest x1 46.5 us: body(): lax.all_gather(picked, ('row', 'col'), axis=0, tiled=True)]
    psum x1 -> x0, blocking collectives: 43.1 us -> none  [body(): product_now = lax.psum(weighted_sum(residual, precond), ('row', 'col'))]
    pallas_call x0 -> x1, Pallas kernels: none -> 38.3 us  [body(): pl.pallas_call(functools.partial(kernel, n_row, n_col), out_shape=(out, o...]
    ppermute x12 -> x0, starting transfers between devices: 29.8 us -> none  [from_behind(): return lax.ppermute(x, axis, pairs)]
    dot_general x5 -> x0, matrix products: 21.4 us -> none  [product(): jnp.dot(matrix, vectors, precision=HIGHEST_PRECISION, preferred_element_t...]
    gather x14 -> x0, local copies, waits for them, and re-layouts: 7.94 us -> none  [the longest x1 2.6 us: body(): columns = jnp.take(coarse_inverse, all_primal, axis=1)]
    scatter x12 -> x0, local copies, waits for them, and re-layouts: 7.48 us -> none  [the longest x6 3.74 us: assemble(): south_back = jnp.zeros_like(south_face).at[south_order].set(south_face)]
    ppermute x12 -> x0, waiting for transfers between devices: 5 us -> none  [from_behind(): return lax.ppermute(x, axis, pairs)]
  transfers between devices with their start and end apart: 12 -> 0, of which waited for: 3 -> 0; matrix products, arithmetic and copies ran while one was open for 9% -> 0% of each run, Pallas kernels for 0% -> 0%
where the time goes in v1:
time: 42.7 us; the launch traced here: 42.3 us
  Pallas kernels  38.3 us (90%)
  local copies, waits for them, and re-layouts  2.75 us (6%)
  between operations  1.29 us (3%)
    pallas_call x1, Pallas kernels, body(): pl.pallas_call(functools.partial(kernel, n_row, n_col), out_shape=(out, o...  38.3 us
    unnamed x2, local copies, waits for them, and re-layouts  2.75 us

profile of v1, /device:TPU:0, one launch (start us, length us, event | category | flops | bytes accessed | tf_op | source)
XLA Modules:
  0.0 42.3 jit_solution(14556205717959360760)
XLA Ops:
  1.3 38.3 %shard_map.104 = (f32[8,1024]{1,0:T(8,128)}, f32[8,1024]{1,0:T(8,128)}) custom-call(f32[8,1024]{1,0:T(8,128)} %bitcast.17, f32[1024,1024]{1,0:T(8,128)} %bitcast.15, f32[1024,1024]{1,0:T(8,128)} %bitcast.16, f32[48,1536]{1,0:T(8,128)} %coarse_hbm.1, s32[1,1]{1,0:T(1,128)S(6)} %copy.13.elements, s32[1,256]{1,0:T(1,128)} %bitcast.20, s32[1,256]{1,0:T(1,128)} %bitcast.21, ...), custom_call_target="tpu_custom_call" | custom-call | tf_op jit(solution)/shard_map/pallas_call | solution.py:345
  39.6 1.4 %copy.14 = f32[1,1,1024,8]{2,3,1,0:T(8,128)} copy(f32[1,1,1024,8]{2,3,1,0:T(8,128)} %bitcast.19) | data formatting | bytes 65536
  41.0 1.4 %copy.15 = f32[1,1,1024,8]{2,3,1,0:T(8,128)} copy(f32[1,1,1024,8]{2,3,1,0:T(8,128)} %bitcast.18) | data formatting | bytes 65536

commit v2 on v1

v2 whole, which is shorter than its diff:
```python
import functools

import jax
import jax.numpy as jnp
from jax import lax
from jax.experimental import pallas as pl
from jax.experimental.pallas import tpu as pltpu
from jax.sharding import PartitionSpec as P

ELEM_BASE = 4096
MOST_SWEEPS = 3
MESH = pl.DeviceIdType.MESH
F32, BF16 = jnp.float32, jnp.bfloat16
NT = (((1,), (1,)), ((), ()))
IDX, RHS, SOL, SUM = range(4)


def split(values):
    high = values.astype(BF16).astype(F32)
    return jnp.concatenate([high, values - high], axis=0).astype(BF16)


def join(stacked):
    rows = stacked.shape[0] // 2
    return stacked[:rows] + stacked[rows:]


def one_hot(numbers, wanted):
    return jnp.where(numbers == wanted, 1.0, 0.0).astype(BF16)


def dot(a, b):
    return jnp.dot(a, b, preferred_element_type=F32)


def dot_nt(a, b):
    return lax.dot_general(a, b, NT, preferred_element_type=F32)


def kernel(
    n_row, n_col, loads, schur_hbm, factor_hbm, coarse_hbm, elements, west_map, south_map,
    prim_local, prim_coarse, direction, image_out, loads_out, alpha_out,
    schur_in, factor_in, coarse_in, schur_hi, schur_lo, factor_hi, factor_lo,
    coarse_split, columns, west_hot, south_hot, local_hot, coarse_hot,
    place, idx_all, val_all, sum_all, face_out, face_in,
    copy_sem, face_send, face_recv, all_send, all_recv,
):
    a, c = lax.axis_index("row"), lax.axis_index("col")
    unknowns = loads.shape[1]
    face = unknowns // 4
    wide = local_hot.shape[1]
    half = wide // 2
    count = n_row * n_col
    me = a * n_col + c
    odd = lax.rem(me, 2)
    coarse_rows, coarse_all = coarse_in.shape
    nprim = prim_local.shape[1]

    copies = [
        pltpu.make_async_copy(src, dst, copy_sem.at[i])
        for i, (src, dst) in enumerate(
            [(factor_hbm, factor_in), (coarse_hbm, coarse_in), (schur_hbm, schur_in)]
        )
    ]
    barrier = pltpu.get_barrier_semaphore()
    def peer(d):
        other = lax.rem(me + d, count)
        return (lax.div(other, n_col), lax.rem(other, n_col))

    def each(work):
        if count <= 64:
            for d in range(1, count):
                work(d)
        else:
            lax.fori_loop(1, count, lambda d, carry: (work(d), carry)[1], 0)

    each(lambda d: pl.semaphore_signal(barrier, inc=1, device_id=peer(d), device_id_type=MESH))
    for copy in copies:
        copy.start()

    def hot(order_ref):
        return one_hot(lax.broadcasted_iota(jnp.int32, (face, face), 0), order_ref[...])

    west_hot[...] = hot(west_map)
    south_hot[...] = hot(south_map)

    def placed(source):
        place[...] = jnp.full(place.shape, -1, jnp.int32)
        place[:1, :nprim] = source[...]
        base = place[...]
        return jnp.where(odd == 1, pltpu.roll(base, half, 1), base)[:1]

    own_coarse = placed(prim_coarse)
    own_local = placed(prim_local)
    idx_all[me] = own_coarse

    lane = lax.broadcasted_iota(jnp.int32, (1, unknowns), 1)
    flags = [c > 0, c < n_col - 1, a > 0, a < n_row - 1]
    halves = [jnp.where(flag, 0.5, 1.0).astype(F32) for flag in flags]
    weights = jnp.where(
        lane < face,
        halves[0],
        jnp.where(lane < 2 * face, halves[1], jnp.where(lane < 3 * face, halves[2], halves[3])),
    )
    targets = [(a, c + 1), (a, c - 1), (a + 1, c), (a - 1, c)]
    can_send = [flags[1], flags[0], flags[3], flags[2]]

    def face_copy(turn, slot):
        return pltpu.make_async_remote_copy(
            src_ref=face_out.at[turn, slot],
            dst_ref=face_in.at[turn, slot],
            send_sem=face_send.at[turn, slot],
            recv_sem=face_recv.at[turn, slot],
            device_id=targets[slot],
            device_id_type=MESH,
        )

    def face_fill(turn, values):
        face_out[turn, 0] = values[:, face : 2 * face]
        face_out[turn, 2] = values[:, 3 * face :]
        face_out[turn, 1] = join(dot_nt(split(values[:, :face]), west_hot[...]))
        face_out[turn, 3] = join(dot_nt(split(values[:, 2 * face : 3 * face]), south_hot[...]))

    def face_start(turn):
        for slot in range(4):
            @pl.when(can_send[slot])
            def _():
                face_copy(turn, slot).start()

    def face_finish(turn, values):
        for slot in range(4):
            @pl.when(flags[slot])
            def _():
                face_copy(turn, slot).wait_recv()

            @pl.when(jnp.logical_not(flags[slot]))
            def _():
                face_in[turn, slot] = jnp.zeros(face_in.shape[2:], F32)
        adds = [
            join(dot(split(face_in[turn, 0]), west_hot[...])),
            face_in[turn, 1],
            join(dot(split(face_in[turn, 2]), south_hot[...])),
            face_in[turn, 3],
        ]
        return values + jnp.concatenate(adds, axis=1)

    def all_copy(buffer, kind, d):
        return pltpu.make_async_remote_copy(
            src_ref=buffer.at[me],
            dst_ref=buffer.at[me],
            send_sem=all_send.at[kind, d],
            recv_sem=all_recv.at[kind, d],
            device_id=peer(d),
            device_id_type=MESH,
        )

    def start(buffer, kind):
        each(lambda d: all_copy(buffer, kind, d).start())

    def arrive(buffer, kind):
        each(lambda d: all_copy(buffer, kind, d).wait_recv())

    def pairs(buffer, s, merge):
        return jnp.concatenate(
            [merge(buffer[4 * s + 2 * i], buffer[4 * s + 2 * i + 1]) for i in range(2)], axis=1
        )

    first = loads[...]
    face_fill(0, first)
    pl.semaphore_wait(barrier, count - 1)
    face_start(0)
    start(idx_all, IDX)

    rows_iota = lax.broadcasted_iota(jnp.int32, (unknowns, wide), 0)
    local_hot[...] = one_hot(rows_iota, own_local)

    def split_matrix(source, high, low):
        step = 128

        def one(i, carry):
            at = pl.ds(pl.multiple_of(i * step, step), step)
            values = source[at, :]
            top = values.astype(BF16)
            high[at, :] = top
            low[at, :] = (values - top.astype(F32)).astype(BF16)
            return carry

        lax.fori_loop(0, source.shape[0] // step, one, 0)

    copies[0].wait()
    split_matrix(factor_in, factor_hi, factor_lo)

    right_side = face_finish(0, first)
    scaled = weights * right_side
    val_all[0, me] = join(dot(split(scaled), local_hot[...]))
    start(val_all.at[0], RHS)

    def apply(high, low, vectors):
        both = split(vectors)
        return join(dot(both, high[...]) + dot(both, low[...]))

    local = apply(factor_hi, factor_lo, scaled)

    copies[1].wait()
    values = coarse_in[...]
    top = values.astype(BF16)
    coarse_split[...] = jnp.zeros(coarse_split.shape, BF16)
    coarse_split[:coarse_rows, :] = top
    coarse_split[half : half + coarse_rows, :] = (values - top.astype(F32)).astype(BF16)
    arrive(idx_all, IDX)
    chunk = 256
    chunks = coarse_all // chunk
    small = lax.broadcasted_iota(jnp.int32, (chunk, 2 * wide), 0).astype(F32).astype(BF16)

    def one_column(s, carry):
        wanted = pairs(idx_all, s, jnp.maximum)

        def one_chunk(k, acc):
            start_at = k * chunk
            offset = wanted - start_at
            inside = jnp.logical_and(offset >= 0, offset < chunk)
            offset = jnp.where(inside, offset, -1).astype(F32).astype(BF16)
            picks = jnp.where(small == offset, jnp.ones_like(small), jnp.zeros_like(small))
            return acc + dot(coarse_split[:, pl.ds(start_at, chunk)], picks)

        acc = jnp.zeros((wide, 2 * wide), F32)
        if chunks <= 8:
            for k in range(chunks):
                acc = one_chunk(k, acc)
        else:
            acc = lax.fori_loop(
                0, chunks, lambda k, acc: one_chunk(pl.multiple_of(k, 1), acc), acc
            )
        values = join(acc)
        top = values.astype(BF16)
        at = pl.ds(pl.multiple_of(s * 2 * wide, 2 * wide), 2 * wide)
        columns[:half, at] = top
        columns[half:, at] = (values - top.astype(F32)).astype(BF16)
        return carry

    lax.fori_loop(0, count // 4, one_column, 0)

    def gathered(buffer):
        return split(
            jnp.concatenate([pairs(buffer, s, jnp.add) for s in range(count // 4)], axis=1)
        )

    arrive(val_all.at[0], RHS)
    solved = join(dot_nt(gathered(val_all.at[0]), columns[...]))
    solved = solved + pltpu.roll(solved, half, 1)
    wide_lane = lax.broadcasted_iota(jnp.int32, solved.shape, 1)
    lowest = odd * half
    mine = jnp.logical_and(wide_lane >= lowest, wide_lane < lowest + half)
    val_all[1, me] = jnp.where(mine, solved, 0.0)
    start(val_all.at[1], SOL)

    copies[2].wait()
    split_matrix(schur_in, schur_hi, schur_lo)

    at = lax.broadcasted_iota(jnp.int32, (wide, wide), 0)
    upper = (at >= half).astype(jnp.int32)
    number = upper * coarse_rows + at - upper * half
    number = jnp.where(at - upper * half < coarse_rows, number, -2 * coarse_all)

    def one_pick(s, carry):
        coarse_hot[pl.ds(pl.multiple_of(s * wide, wide), wide), :] = one_hot(
            number, own_coarse - s * 2 * coarse_rows
        )
        return carry

    lax.fori_loop(0, count // 2, one_pick, 0)

    for turn in range(2, MOST_SWEEPS + 1):
        inner = scaled - apply(schur_hi, schur_lo, local)
        later = local + apply(factor_hi, factor_lo, inner)
        more = jnp.broadcast_to(elements[...], local.shape) >= turn * ELEM_BASE
        local = jnp.where(more, later, local)

    arrive(val_all.at[1], SOL)
    read = join(dot(gathered(val_all.at[1]), coarse_hot[...]))
    correction = join(dot_nt(split(read), local_hot[...]))
    halved = weights * (local + correction)
    face_fill(1, halved)
    face_start(1)

    def lane_sum(values):
        return jnp.sum(values, axis=1, keepdims=True)

    rz = lane_sum(right_side * halved)
    precond = face_finish(1, halved)
    image = apply(schur_hi, schur_lo, precond)
    face_fill(2, image)
    face_start(2)
    pq = lane_sum(precond * image)
    sum_lane = lax.broadcasted_iota(jnp.int32, sum_all.shape[1:], 1)
    sum_all[me] = jnp.where(sum_lane == 0, rz, pq)
    start(sum_all, SUM)
    direction[...] = precond
    loads_out[...] = right_side
    image_out[...] = face_finish(2, image)
    arrive(sum_all, SUM)
    sums = sum_all[0]
    for i in range(1, count):
        sums = sums + sum_all[i]
    alpha_out[...] = jnp.broadcast_to(sums[:, :1] / sums[:, 1:2], alpha_out.shape)

    for kind, buffer in enumerate([idx_all, val_all.at[0], val_all.at[1], sum_all]):
        each(lambda d: all_copy(buffer, kind, d).wait_send())
    for turn in range(3):
        for slot in range(4):
            @pl.when(can_send[slot])
            def _():
                face_copy(turn, slot).wait_send()


def up(n, to):
    return -(-n // to) * to


def body(
    n_row, n_col, loads, schur, factor, coarse_inverse, elements, west_map, south_map,
    prim_local, prim_coarse,
):
    vectors = loads[0, 0].T
    rhs, unknowns = vectors.shape
    face = unknowns // 4
    coarse_rows, coarse_all = coarse_inverse.shape
    nprim = prim_local.shape[2]
    wide = 2 * up(max(nprim, coarse_rows), 64)
    count = n_row * n_col
    vmem = pl.BlockSpec(memory_space=pltpu.VMEM)
    hbm = pl.BlockSpec(memory_space=pl.ANY)
    dma = pltpu.SemaphoreType.DMA
    out = jax.ShapeDtypeStruct(vectors.shape, F32)
    direction, image, right_side, alpha = pl.pallas_call(
        functools.partial(kernel, n_row, n_col),
        out_shape=(out, out, out, out),
        in_specs=[vmem, hbm, hbm, hbm, vmem, vmem, vmem, vmem, vmem],
        out_specs=(vmem, vmem, vmem, vmem),
        scratch_shapes=[
            pltpu.VMEM((unknowns, unknowns), F32),
            pltpu.VMEM((unknowns, unknowns), F32),
            pltpu.VMEM((coarse_rows, coarse_all), F32),
            pltpu.VMEM((unknowns, unknowns), BF16),
            pltpu.VMEM((unknowns, unknowns), BF16),
            pltpu.VMEM((unknowns, unknowns), BF16),
            pltpu.VMEM((unknowns, unknowns), BF16),
            pltpu.VMEM((wide, coarse_all), BF16),
            pltpu.VMEM((wide, count // 2 * wide), BF16),
            pltpu.VMEM((face, face), BF16),
            pltpu.VMEM((face, face), BF16),
            pltpu.VMEM((unknowns, wide), BF16),
            pltpu.VMEM((count // 2 * wide, wide), BF16),
            pltpu.VMEM((8, wide), jnp.int32),
            pltpu.VMEM((count, 1, wide), jnp.int32),
            pltpu.VMEM((2, count, rhs, wide), F32),
            pltpu.VMEM((count, rhs, 128), F32),
            pltpu.VMEM((3, 4, rhs, face), F32),
            pltpu.VMEM((3, 4, rhs, face), F32),
            dma((3,)),
            dma((3, 4)),
            dma((3, 4)),
            dma((4, count)),
            dma((4, count)),
        ],
        compiler_params=pltpu.CompilerParams(collective_id=0, has_side_effects=True),
    )(
        vectors, schur[0, 0], factor[0, 0], coarse_inverse, elements,
        west_map[0], south_map[0], prim_local[0], prim_coarse[0],
    )
    solution = alpha * direction
    residual = right_side - alpha * image
    return solution.T[None, None], residual.T[None, None]


def solution(mesh):
    placed = (
        P("row", "col", None, None),
        P("row", "col", None, None),
        P("row", "col", None, None),
        P(("row", "col"), None),
        P("row", "col"),
        P("row", "col", None),
        P("row", "col", None),
        P("row", "col", None),
        P("row", "col", None),
    )
    return jax.shard_map(
        functools.partial(body, mesh.shape["row"], mesh.shape["col"]),
        mesh=mesh,
        in_specs=placed,
        out_specs=(P("row", "col", None, None), P("row", "col", None, None)),
        check_vma=False,
    )
```

time: 42.7 us -> 37.3 us (0.87)
  Pallas kernels: 38.3 us -> 34.4 us
  local copies, waits for them, and re-layouts: 2.75 us -> 0 us
  other arithmetic: 0 us -> 1.44 us
    pallas_call x1, Pallas kernels: 38.3 us -> 34.4 us  [body(): pl.pallas_call(functools.partial(kernel, n_row, n_col), out_shape=(out, o...]
    unnamed x2 -> x0, local copies, waits for them, and re-layouts: 2.75 us -> none
    broadcast_in_dim x0 -> x1, other arithmetic: none -> 1.44 us  [body(): return (solution.T[None, None], residual.T[None, None])]
where the time goes in v2:
time: 37.3 us; the launch traced here: 37.1 us
  Pallas kernels  34.4 us (92%)
  other arithmetic  1.44 us (4%)
  between operations  1.29 us (3%)
    pallas_call x1, Pallas kernels, body(): pl.pallas_call(functools.partial(kernel, n_row, n_col), out_shape=(out, o...  34.4 us
    broadcast_in_dim x1, other arithmetic, body(): return (solution.T[None, None], residual.T[None, None])  1.44 us

profile of v2, /device:TPU:0, one launch (start us, length us, event | category | flops | bytes accessed | tf_op | source)
XLA Modules:
  0.0 37.1 jit_solution(6108152237063122423)
XLA Ops:
  1.3 34.4 %shard_map.104 = (f32[8,1024]{1,0:T(8,128)}, f32[8,1024]{1,0:T(8,128)}, f32[8,1024]{1,0:T(8,128)}, f32[8,1024]{1,0:T(8,128)}) custom-call(f32[8,1024]{1,0:T(8,128)} %bitcast.19, f32[1024,1024]{1,0:T(8,128)} %bitcast.17, f32[1024,1024]{1,0:T(8,128)} %bitcast.18, f32[48,1536]{1,0:T(8,128)} %coarse_hbm.1, s32[1,1]{1,0:T(1,128)S(6)} %copy.11.elements, ...), custom_call_target="tpu_custom_call" | custom-call | tf_op jit(solution)/shard_map/pallas_call | solution.py:335
  35.6 1.4 %subtract_bitcast_fusion = (f32[1,1,1024,8]{2,3,1,0:T(8,128)}, f32[1,1,1024,8]{2,3,1,0:T(8,128)}) fusion(f32[8,1024]{1,0:T(8,128)} %get-tuple-element.8, f32[8,1024]{1,0:T(8,128)} %get-tuple-element.6, f32[8,1024]{1,0:T(8,128)} %get-tuple-element.9, f32[8,1024]{1,0:T(8,128)} %get-tuple-element.7), kind=kLoop, calls=%fused_computation | loop fusion | flops 24576 | bytes 196608 | tf_op jit(solution)/shard_map/broadcast_in_dim | solution.py:373

commit v3 on v2

--- a/solution.py
+++ b/solution.py
@@ -88,10 +88,11 @@
         place[...] = jnp.full(place.shape, -1, jnp.int32)
         place[:1, :nprim] = source[...]
         base = place[...]
-        return jnp.where(odd == 1, pltpu.roll(base, half, 1), base)[:1]
-
-    own_coarse = placed(prim_coarse)
-    own_local = placed(prim_local)
+        return base, pltpu.roll(base, half, 1)
+
+    base, rolled = placed(prim_coarse)
+    own_coarse = jnp.where(odd == 1, rolled, base)[:1]
+    own_local = jnp.maximum(*placed(prim_local))[:1]
     idx_all[me] = own_coarse
 
     lane = lax.broadcasted_iota(jnp.int32, (1, unknowns), 1)
@@ -160,10 +161,18 @@
     def arrive(buffer, kind):
         each(lambda d: all_copy(buffer, kind, d).wait_recv())
 
-    def pairs(buffer, s, merge):
-        return jnp.concatenate(
-            [merge(buffer[4 * s + 2 * i], buffer[4 * s + 2 * i + 1]) for i in range(2)], axis=1
-        )
+    rhs = loads.shape[0]
+    lower = lax.broadcasted_iota(jnp.int32, (rhs // 2, wide), 1) < half
+
+    def pack(values):
+        return jnp.where(lower, values[: rhs // 2], values[rhs // 2 :])
+
+    def unpack(first, second):
+        both = jnp.concatenate([first, second], axis=0)
+        swapped = pltpu.roll(both, half, 1)
+        top = jnp.where(lower, both[: rhs // 2], swapped[rhs // 2 :])
+        bottom = jnp.where(lower, swapped[: rhs // 2], both[rhs // 2 :])
+        return jnp.concatenate([top, bottom], axis=0)
 
     first = loads[...]
     face_fill(0, first)
@@ -192,7 +201,7 @@
 
     right_side = face_finish(0, first)
     scaled = weights * right_side
-    val_all[0, me] = join(dot(split(scaled), local_hot[...]))
+    val_all[0, me] = pack(join(dot(split(scaled), local_hot[...])))
     start(val_all.at[0], RHS)
 
     def apply(high, low, vectors):
@@ -213,7 +222,9 @@
     small = lax.broadcasted_iota(jnp.int32, (chunk, 2 * wide), 0).astype(F32).astype(BF16)
 
     def one_column(s, carry):
-        wanted = pairs(idx_all, s, jnp.maximum)
+        wanted = jnp.concatenate(
+            [jnp.maximum(idx_all[4 * s + i], idx_all[4 * s + i + 1]) for i in (0, 2)], axis=1
+        )
 
         def one_chunk(k, acc):
             start_at = k * chunk
@@ -242,16 +253,13 @@
 
     def gathered(buffer):
         return split(
-            jnp.concatenate([pairs(buffer, s, jnp.add) for s in range(count // 4)], axis=1)
+            jnp.concatenate([unpack(buffer[s], buffer[s + 1]) for s in range(0, count, 2)], axis=1)
         )
 
     arrive(val_all.at[0], RHS)
     solved = join(dot_nt(gathered(val_all.at[0]), columns[...]))
     solved = solved + pltpu.roll(solved, half, 1)
-    wide_lane = lax.broadcasted_iota(jnp.int32, solved.shape, 1)
-    lowest = odd * half
-    mine = jnp.logical_and(wide_lane >= lowest, wide_lane < lowest + half)
-    val_all[1, me] = jnp.where(mine, solved, 0.0)
+    val_all[1, me] = pack(solved)
     start(val_all.at[1], SOL)
 
     copies[2].wait()
@@ -292,8 +300,11 @@
     face_fill(2, image)
     face_start(2)
     pq = lane_sum(precond * image)
-    sum_lane = lax.broadcasted_iota(jnp.int32, sum_all.shape[1:], 1)
-    sum_all[me] = jnp.where(sum_lane == 0, rz, pq)
+    sum_lane = lax.broadcasted_iota(jnp.int32, (rhs, 128), 1)
+    sum_case = lax.broadcasted_iota(jnp.int32, (rhs, 128), 0)
+    upper_lane, lower_lane = sum_lane == sum_case + rhs, sum_lane == sum_case
+    laid = jnp.where(lower_lane, rz, 0.0) + jnp.where(upper_lane, pq, 0.0)
+    sum_all[me] = jnp.sum(laid, axis=0, keepdims=True)
     start(sum_all, SUM)
     direction[...] = precond
     loads_out[...] = right_side
@@ -302,7 +313,9 @@
     sums = sum_all[0]
     for i in range(1, count):
         sums = sums + sum_all[i]
-    alpha_out[...] = jnp.broadcast_to(sums[:, :1] / sums[:, 1:2], alpha_out.shape)
+    sums = jnp.broadcast_to(sums, (rhs, 128))
+    alpha = lane_sum(jnp.where(lower_lane, sums, 0.0)) / lane_sum(jnp.where(upper_lane, sums, 0.0))
+    alpha_out[...] = jnp.broadcast_to(alpha, alpha_out.shape)
 
     for kind, buffer in enumerate([idx_all, val_all.at[0], val_all.at[1], sum_all]):
         each(lambda d: all_copy(buffer, kind, d).wait_send())
@@ -353,8 +366,8 @@
             pltpu.VMEM((count // 2 * wide, wide), BF16),
             pltpu.VMEM((8, wide), jnp.int32),
             pltpu.VMEM((count, 1, wide), jnp.int32),
-            pltpu.VMEM((2, count, rhs, wide), F32),
-            pltpu.VMEM((count, rhs, 128), F32),
+            pltpu.VMEM((2, count, rhs // 2, wide), F32),
+            pltpu.VMEM((count, 1, 128), F32),
             pltpu.VMEM((3, 4, rhs, face), F32),
             pltpu.VMEM((3, 4, rhs, face), F32),
             dma((3,)),

time: 37.3 us -> 35.7 us (0.957)
  Pallas kernels: 34.4 us -> 32.7 us
    pallas_call x1, Pallas kernels: 34.4 us -> 32.7 us  [body(): pl.pallas_call(functools.partial(kernel, n_row, n_col), out_shape=(out, o...]
where the time goes in v3:
time: 35.7 us; the launch traced here: 35.5 us
  Pallas kernels  32.7 us (92%)
  other arithmetic  1.44 us (4%)
  between operations  1.29 us (4%)
    pallas_call x1, Pallas kernels, body(): pl.pallas_call(functools.partial(kernel, n_row, n_col), out_shape=(out, o...  32.7 us
    broadcast_in_dim x1, other arithmetic, body(): return (solution.T[None, None], residual.T[None, None])  1.44 us

profile of v3, /device:TPU:0, one launch (start us, length us, event | category | flops | bytes accessed | tf_op | source)
XLA Modules:
  0.0 35.5 jit_solution(2274608515078310651)
XLA Ops:
  1.3 32.7 %shard_map.104 = (f32[8,1024]{1,0:T(8,128)}, f32[8,1024]{1,0:T(8,128)}, f32[8,1024]{1,0:T(8,128)}, f32[8,1024]{1,0:T(8,128)}) custom-call(f32[8,1024]{1,0:T(8,128)} %bitcast.19, f32[1024,1024]{1,0:T(8,128)} %bitcast.17, f32[1024,1024]{1,0:T(8,128)} %bitcast.18, f32[48,1536]{1,0:T(8,128)} %coarse_hbm.1, s32[1,1]{1,0:T(1,128)S(6)} %copy.11.elements, ...), custom_call_target="tpu_custom_call" | custom-call | tf_op jit(solution)/shard_map/pallas_call | solution.py:348
  34.0 1.4 %subtract_bitcast_fusion = (f32[1,1,1024,8]{2,3,1,0:T(8,128)}, f32[1,1,1024,8]{2,3,1,0:T(8,128)}) fusion(f32[8,1024]{1,0:T(8,128)} %get-tuple-element.8, f32[8,1024]{1,0:T(8,128)} %get-tuple-element.6, f32[8,1024]{1,0:T(8,128)} %get-tuple-element.9, f32[8,1024]{1,0:T(8,128)} %get-tuple-element.7), kind=kLoop, calls=%fused_computation | loop fusion | flops 24576 | bytes 196608 | tf_op jit(solution)/shard_map/broadcast_in_dim | solution.py:386

commit v4 on v3

--- a/solution.py
+++ b/solution.py
@@ -297,8 +297,6 @@
     rz = lane_sum(right_side * halved)
     precond = face_finish(1, halved)
     image = apply(schur_hi, schur_lo, precond)
-    face_fill(2, image)
-    face_start(2)
     pq = lane_sum(precond * image)
     sum_lane = lax.broadcasted_iota(jnp.int32, (rhs, 128), 1)
     sum_case = lax.broadcasted_iota(jnp.int32, (rhs, 128), 0)
@@ -306,6 +304,8 @@
     laid = jnp.where(lower_lane, rz, 0.0) + jnp.where(upper_lane, pq, 0.0)
     sum_all[me] = jnp.sum(laid, axis=0, keepdims=True)
     start(sum_all, SUM)
+    face_fill(2, image)
+    face_start(2)
     direction[...] = precond
     loads_out[...] = right_side
     image_out[...] = face_finish(2, image)

time: 35.7 us -> 35.6 us (level)
  no operation moved by 1% of the time
where the time goes in v4:
time: 35.6 us; the launch traced here: 35.3 us
  Pallas kernels  32.6 us (92%)
  other arithmetic  1.44 us (4%)
  between operations  1.29 us (4%)
    pallas_call x1, Pallas kernels, body(): pl.pallas_call(functools.partial(kernel, n_row, n_col), out_shape=(out, o...  32.6 us
    broadcast_in_dim x1, other arithmetic, body(): return (solution.T[None, None], residual.T[None, None])  1.44 us

profile of v4, /device:TPU:0, one launch (start us, length us, event | category | flops | bytes accessed | tf_op | source)
XLA Modules:
  0.0 35.3 jit_solution(13163997689254054970)
XLA Ops:
  1.3 32.6 %shard_map.104 = (f32[8,1024]{1,0:T(8,128)}, f32[8,1024]{1,0:T(8,128)}, f32[8,1024]{1,0:T(8,128)}, f32[8,1024]{1,0:T(8,128)}) custom-call(f32[8,1024]{1,0:T(8,128)} %bitcast.19, f32[1024,1024]{1,0:T(8,128)} %bitcast.17, f32[1024,1024]{1,0:T(8,128)} %bitcast.18, f32[48,1536]{1,0:T(8,128)} %coarse_hbm.1, s32[1,1]{1,0:T(1,128)S(6)} %copy.11.elements, ...), custom_call_target="tpu_custom_call" | custom-call | tf_op jit(solution)/shard_map/pallas_call | solution.py:348
  33.9 1.4 %subtract_bitcast_fusion = (f32[1,1,1024,8]{2,3,1,0:T(8,128)}, f32[1,1,1024,8]{2,3,1,0:T(8,128)}) fusion(f32[8,1024]{1,0:T(8,128)} %get-tuple-element.8, f32[8,1024]{1,0:T(8,128)} %get-tuple-element.6, f32[8,1024]{1,0:T(8,128)} %get-tuple-element.9, f32[8,1024]{1,0:T(8,128)} %get-tuple-element.7), kind=kLoop, calls=%fused_computation | loop fusion | flops 24576 | bytes 196608 | tf_op jit(solution)/shard_map/broadcast_in_dim | solution.py:386
